TPU v7x, 512 devices: a whole 4x8x8 slice. The times are simulated.
512 devices in a mesh: gz: 128 (over y, z, core), gx: 4 (over x).
Axes of the slice: x: 4, y: 8, z: 8, core: 2. Of those that a mesh axis runs over, the one named last changes fastest.
Arguments:
- velocity: float32 [3, 6, 2048, 4096], P(None, None, 'gz', 'gx'), may hold values from -6 to 6
- colormap: float32 [8, 16, 4], replicated, may hold values from 0 to 1
- map_choice: int32 [4, 4096], P(None, 'gx'), may hold values from 0 to 7
Outputs:
- image: float32 [4, 4, 4096], P(None, None, ('gx', 'gz'))
All inputs are finite; a program needn't handle non-finite values.
Results may differ from a plain program's by a relative error of at most 0.0003.
Values sent between devices are 32-bit elements; how exact they have to be, the bound alone decides.
No kernel may reach another device: no remote copies, remote signals or barrier semaphores. Data moves between devices by JAX's collectives and lax.ppermute only.
A program may use at most 64 MiB of HBM per device.

v0:
```python
import jax
import jax.numpy as jnp
from jax import lax
from jax.sharding import PartitionSpec as P


def shift(x, axis, step):
    count = lax.axis_size(axis)
    return lax.ppermute(x, axis, [(i, (i + step) % count) for i in range(count)])


def shade(velocity, z_low, z_high, x_low, x_high, palette, depth_total):
    mid = velocity[:, 1:-1]
    along_y = (velocity[:, 2:] - velocity[:, :-2]) * 0.5
    in_z = jnp.concatenate([z_low, mid, z_high], axis=2)
    along_z = (in_z[:, :, 2:] - in_z[:, :, :-2]) * 0.5
    in_x = jnp.concatenate([x_low, mid, x_high], axis=3)
    along_x = (in_x[..., 2:] - in_x[..., :-2]) * 0.5
    derivs = (along_x, along_y, along_z)
    criterion = jnp.zeros_like(along_x[0])
    for component in range(3):
        for direction in range(3):
            criterion = criterion + derivs[direction][component] * derivs[component][direction]
    criterion = -0.5 * criterion
    knot_count = palette.shape[0]
    position = (knot_count - 1) * jax.nn.sigmoid(criterion)
    colours = [jnp.zeros_like(criterion) for channel in range(4)]
    for knot_index in range(knot_count):
        weight = jnp.maximum(0.0, 1.0 - jnp.abs(position - knot_index))
        for channel in range(4):
            colours[channel] = colours[channel] + weight * palette[knot_index, channel][:, None, :]
    kept = jnp.exp(-4.0 * colours[3] / depth_total)
    before = jnp.ones_like(kept[:, 0])
    colour = [jnp.zeros_like(before) for channel in range(3)]
    for z in range(kept.shape[1]):
        weight_z = before * (1.0 - kept[:, z])
        for channel in range(3):
            colour[channel] = colour[channel] + weight_z * colours[channel][:, z]
        before = before * kept[:, z]
    return jnp.stack(colour + [before])


def on_device(velocity, colormap, map_choice):
    slabs = lax.axis_size("gz")
    depth_total = velocity.shape[2] * slabs
    map_count = colormap.shape[0]
    mid = velocity[:, 1:-1]
    z_low = shift(mid[:, :, -1:], "gz", 1)
    z_high = shift(mid[:, :, :1], "gz", -1)
    x_low = shift(mid[..., -1:], "gx", 1)
    x_high = shift(mid[..., :1], "gx", -1)
    selector = (map_choice[:, :, None] == jnp.arange(map_count, dtype=jnp.int32)).astype(
        jnp.float32
    )
    flat_rows = jnp.dot(
        selector.reshape(-1, map_count),
        colormap.reshape(map_count, -1),
        precision=lax.Precision.HIGHEST,
        preferred_element_type=jnp.float32,
    )
    palette = jnp.transpose(flat_rows.reshape(map_choice.shape + colormap.shape[1:]), (2, 3, 0, 1))
    terms = shade(velocity, z_low, z_high, x_low, x_high, palette, depth_total)
    channels, rows, columns = terms.shape
    share = columns // slabs
    parts = terms.reshape(channels * rows, slabs, share).transpose(1, 0, 2)
    parts = parts.reshape(slabs, channels * rows * share)
    seen = lax.all_to_all(parts, "gz", 0, 0, tiled=True).reshape(slabs, channels, rows * share)
    ahead = jnp.cumprod(seen[:, 3], axis=0)
    before = jnp.concatenate([jnp.ones_like(ahead[:1]), ahead[:-1]], axis=0)
    image = jnp.sum(before[:, None] * seen[:, :3], axis=0)
    image = jnp.concatenate([image, 1.0 - ahead[-1:]], axis=0)
    return image.reshape(channels, rows, share)


def solution(mesh):
    placed = (P(None, None, "gz", "gx"), P(), P(None, "gx"))
    return jax.shard_map(
        on_device,
        mesh=mesh,
        in_specs=placed,
        out_specs=P(None, None, ("gx", "gz")),
        check_vma=False,
    )
```

profile of v0, /device:TPU:1, one launch (start us, length us, event | category | flops | bytes accessed | tf_op | source)
XLA Modules:
  0.0 58.2 jit_solution(2748639414874757181)
XLA Ops:
  0.0 1.2 %fusion.146 = (f32[3,4,1,1024]{3,2,1,0:T(1,128)S(1)}, f32[3,4,1,1024]{3,2,1,0:T(1,128)S(1)}) fusion(f32[3,6,16,1024]{3,2,1,0:T(8,128)} %param.3), kind=kLoop, calls=%fused_computation.320 | loop fusion | bytes 196608 | tf_op jit(solution)/shard_map/slice | solution.py:49
  1.2 8.7 %collective-permute-start.2 = (f32[3,4,1,1024]{3,2,1,0:T(1,128)S(1)}, f32[3,4,1,1024]{3,2,1,0:T(1,128)S(1)}, u32[]{:S(2)}, u32[]{:S(2)}) collective-permute-start(f32[3,4,1,1024]{3,2,1,0:T(1,128)S(1)} %get-tuple-element.26), channel_id=1, source_target_pairs={{0,508},{4,0},{8,4},{12,8},{16,12},{20,16},{24,20},{28,24},{32,28}... | collective-permute-start | bytes 147464 | tf_op jit(solution)/shard_map/ppermute | solution.py:9
  9.9 1.9 %collective-permute-start.3 = (f32[3,4,1,1024]{3,2,1,0:T(1,128)S(1)}, f32[3,4,1,1024]{3,2,1,0:T(1,128)S(1)}, u32[]{:S(2)}, u32[]{:S(2)}) collective-permute-start(f32[3,4,1,1024]{3,2,1,0:T(1,128)S(1)} %get-tuple-element.27), channel_id=1, source_target_pairs={{0,4},{4,8},{8,12},{12,16},{16,20},{20,24},{24,28},{28,32},{32,36}... | collective-permute-start | bytes 147464 | tf_op jit(solution)/shard_map/ppermute | solution.py:9
  11.9 1.0 %fusion.145 = (f32[3,4,16,1]{3,2,1,0:T(8,128)S(1)}, f32[3,4,16,1]{3,2,1,0:T(8,128)S(1)}) fusion(f32[3,6,16,1024]{3,2,1,0:T(8,128)} %param.3), kind=kLoop, calls=%fused_computation.319 | loop fusion | bytes 3072 | tf_op jit(solution)/shard_map/slice | solution.py:51
  12.9 1.9 %collective-permute-start = (f32[3,4,16,1]{3,2,1,0:T(8,128)S(1)}, f32[3,4,16,1]{3,2,1,0:T(8,128)S(1)}, u32[]{:S(2)}, u32[]{:S(2)}) collective-permute-start(f32[3,4,16,1]{3,2,1,0:T(8,128)S(1)} %get-tuple-element.22), channel_id=1, source_target_pairs={{0,3},{1,0},{2,1},{3,2},{4,7},{5,4},{6,5},{7,6},{8,11},{9,8},{10,9... | collective-permute-start | bytes 2312 | tf_op jit(solution)/shard_map/ppermute | solution.py:9
  14.8 3.4 %collective-permute-start.1 = (f32[3,4,16,1]{3,2,1,0:T(8,128)S(1)}, f32[3,4,16,1]{3,2,1,0:T(8,128)S(1)}, u32[]{:S(2)}, u32[]{:S(2)}) collective-permute-start(f32[3,4,16,1]{3,2,1,0:T(8,128)S(1)} %get-tuple-element.23), channel_id=1, source_target_pairs={{0,1},{1,2},{2,3},{3,0},{4,5},{5,6},{6,7},{7,4},{8,9},{9,10},{10,1... | collective-permute-start | bytes 2312 | tf_op jit(solution)/shard_map/ppermute | solution.py:9
  18.2 1.4 %convolution_bitcast_fusion = f32[16,4,4,1024]{3,0,1,2:T(8,128)S(1)} fusion(s32[4,1024]{1,0:T(4,128)} %param.5, f32[16,4,8]{0,1,2:T(4,128)} %bitcast.815), kind=kOutput, calls=%fused_computation | convolution fusion | flops 25198592 | bytes 1067008 | tf_op jit(solution)/shard_map/dot_general | solution.py:55
  19.6 0.1 fusion.150
  19.7 0.3 fusion.147
  20.0 0.3 fusion.148
  20.3 0.3 fusion.149
  20.6 0.3 copy-done
  20.9 0.2 subtract_multiply_fusion
  21.7 0.7 %fusion.3 = (f32[3,4,16,1024]{3,2,1,0:T(8,128)S(1)}, f32[3,4,16,1024]{3,2,1,0:T(8,128)S(1)}) fusion(f32[3,4,16,1024]{3,2,1,0:T(8,128)S(1)} %get-tuple-element.25, f32[3,4,16,1]{3,2,1,0:T(8,128)S(1)} %collective-permute-done.1, f32[3,4,16,1]{3,2,1,0:T(8,128)S(1)} %collective-permute-done, f32[3,4,1,1024]{3,2,1,0:T(1,128)S(1)} %collective-permute-done.3, ...), kind=kLoop, calls=%fused_computation.7 | loop fusion | flops 1572864 | bytes 2459136 | tf_op jit(solution)/shard_map/mul | solution.py:18
  22.3 1.0 %multiply_add_fusion.2 = (f32[4,16,1024]{2,1,0:T(8,128)S(1)}, f32[4,16,1024]{2,1,0:T(8,128)S(1)}) fusion(f32[4,1024]{1,0:T(4,128)S(1)} %get-tuple-element.130, f32[4,1024]{1,0:T(4,128)S(1)} %get-tuple-element.131, f32[4,1024]{1,0:T(4,128)S(1)} %get-tuple-element.132, f32[4,1024]{1,0:T(4,128)S(1)} %get-tuple-element.133, ...), kind=kLoop, calls=%fused_computation.37 | loop fusion | flops 7405568 | bytes 3145728 | tf_op jit(solution)/shard_map/add | solution.py:31
  23.3 0.8 %multiply_exponential_fusion = f32[4,16,1024]{2,1,0:T(8,128)S(1)} fusion(f32[4,1024]{1,0:T(4,128)S(1)} %get-tuple-element.104, f32[4,1024]{1,0:T(4,128)S(1)} %get-tuple-element.105, f32[4,1024]{1,0:T(4,128)S(1)} %get-tuple-element.106, f32[4,1024]{1,0:T(4,128)S(1)} %get-tuple-element.107, f32[4,1024]{1,0:T(4,128)S(1)} %get-tuple-element.108, ...), kind=kLoop, calls=%fused_computation.38 | loop fusion | flops 6225920 | bytes 786432 | tf_op jit(solution)/shard_map/exp | solution.py:32
  24.2 0.6 fusion.91
  24.8 0.8 %multiply_add_fusion = f32[4,16,1024]{2,1,0:T(8,128)S(1)} fusion(f32[4,1024]{1,0:T(4,128)S(1)} %get-tuple-element.138, f32[4,1024]{1,0:T(4,128)S(1)} %get-tuple-element.139, f32[4,1024]{1,0:T(4,128)S(1)} %get-tuple-element.140, f32[4,1024]{1,0:T(4,128)S(1)} %get-tuple-element.141, f32[4,1024]{1,0:T(4,128)S(1)} %get-tuple-element.142, ...), kind=kLoop, calls=%fused_computation.35 | loop fusion | flops 6160384 | bytes 786432 | tf_op jit(solution)/shard_map/add | solution.py:31
  25.6 0.4 fusion.29
  26.0 0.8 %multiply_add_fusion.1 = f32[4,16,1024]{2,1,0:T(8,128)S(1)} fusion(f32[4,1024]{1,0:T(4,128)S(1)} %get-tuple-element.154, f32[4,1024]{1,0:T(4,128)S(1)} %get-tuple-element.155, f32[4,1024]{1,0:T(4,128)S(1)} %get-tuple-element.118, f32[4,1024]{1,0:T(4,128)S(1)} %get-tuple-element.119, f32[4,1024]{1,0:T(4,128)S(1)} %get-tuple-element.120, ...), kind=kLoop, calls=%fused_computation.36 | loop fusion | flops 6160384 | bytes 786432 | tf_op jit(solution)/shard_map/add | solution.py:31
  26.8 0.4 fusion.60
  27.2 0.1 pad_maximum_fusion.4
  27.3 0.6 %reshape.1368 = f32[16,128,8]{2,1,0:T(8,128)S(1)} reshape(f32[4,4,1024]{2,1,0:T(4,128)S(1)} %copy.12) | data formatting | bytes 131072 | tf_op jit(solution)/shard_map/reshape | solution.py:65
  27.9 0.3 copy.13
  28.2 0.1 copy.14
  28.3 28.5 %all_to_all.9 = f32[128,1,128]{2,1,0:T(1,128)S(1)} all-to-all(f32[128,1,128]{2,1,0:T(1,128)S(1)} %copy.14), channel_id=1, replica_groups=mesh['gz'=128,'gx'=4] {'gz'}, dimensions={0} | all-to-all | bytes 131072 | tf_op jit(solution)/shard_map/all_to_all | solution.py:67
  56.8 0.1 copy.15
  56.9 0.1 copy.16
  57.0 0.2 reduce_window.9
  57.3 0.1 concatenate.24.clone
  57.3 0.1 fusion.27
  57.5 0.7 %reshape.1370 = f32[4,4,8]{2,1,0:T(4,128)} reshape(f32[4,32]{1,0:T(4,128)S(1)} %pad_maximum_fusion.5) | data formatting | bytes 1024 | tf_op jit(solution)/shard_map/reshape | solution.py:72
  (43 shorter events, 0.5 us)
Async XLA Ops:
  1.2 20.5 %collective-permute-start.2 = (f32[3,4,1,1024]{3,2,1,0:T(1,128)S(1)}, f32[3,4,1,1024]{3,2,1,0:T(1,128)S(1)}, u32[]{:S(2)}, u32[]{:S(2)}) collective-permute-start(f32[3,4,1,1024]{3,2,1,0:T(1,128)S(1)} %get-tuple-element.26), channel_id=1, source_target_pairs={{0,508},{4,0},{8,4},{12,8},{16,12},{20,16},{24,20},{28,24},{32,28}... | collective-permute-start | bytes 147464 | tf_op jit(solution)/shard_map/ppermute | solution.py:9
  9.9 11.7 %collective-permute-start.3 = (f32[3,4,1,1024]{3,2,1,0:T(1,128)S(1)}, f32[3,4,1,1024]{3,2,1,0:T(1,128)S(1)}, u32[]{:S(2)}, u32[]{:S(2)}) collective-permute-start(f32[3,4,1,1024]{3,2,1,0:T(1,128)S(1)} %get-tuple-element.27), channel_id=1, source_target_pairs={{0,4},{4,8},{8,12},{12,16},{16,20},{20,24},{24,28},{28,32},{32,36}... | collective-permute-start | bytes 147464 | tf_op jit(solution)/shard_map/ppermute | solution.py:9
  12.9 8.7 %collective-permute-start = (f32[3,4,16,1]{3,2,1,0:T(8,128)S(1)}, f32[3,4,16,1]{3,2,1,0:T(8,128)S(1)}, u32[]{:S(2)}, u32[]{:S(2)}) collective-permute-start(f32[3,4,16,1]{3,2,1,0:T(8,128)S(1)} %get-tuple-element.22), channel_id=1, source_target_pairs={{0,3},{1,0},{2,1},{3,2},{4,7},{5,4},{6,5},{7,6},{8,11},{9,8},{10,9... | collective-permute-start | bytes 2312 | tf_op jit(solution)/shard_map/ppermute | solution.py:9
  14.8 6.8 %collective-permute-start.1 = (f32[3,4,16,1]{3,2,1,0:T(8,128)S(1)}, f32[3,4,16,1]{3,2,1,0:T(8,128)S(1)}, u32[]{:S(2)}, u32[]{:S(2)}) collective-permute-start(f32[3,4,16,1]{3,2,1,0:T(8,128)S(1)} %get-tuple-element.23), channel_id=1, source_target_pairs={{0,1},{1,2},{2,3},{3,0},{4,5},{5,6},{6,7},{7,4},{8,9},{9,10},{10,1... | collective-permute-start | bytes 2312 | tf_op jit(solution)/shard_map/ppermute | solution.py:9
  19.6 1.3 %copy-start = (f32[3,6,16,1024]{3,2,1,0:T(8,128)S(1)}, f32[3,6,16,1024]{3,2,1,0:T(8,128)}, u32[]{:S(2)}) copy-start(f32[3,6,16,1024]{3,2,1,0:T(8,128)} %param.3) | copy-start | bytes 3538948
where the time goes:
time: 58.6 us; the launch traced here: 58.2 us
  blocking collectives  28.5 us (49%)
  starting transfers between devices  15.9 us (27%)
  other arithmetic  6.03 us (10%)
  local copies, waits for them, and re-layouts  5.85 us (10%)
  matrix products  1.37 us (2%)
    all_to_all x1, blocking collectives, on_device(): lax.all_to_all(parts, 'gz', 0, 0, tiled=True)  28.5 us
    ppermute x4, starting transfers between devices, shift(): lax.ppermute(x, axis, [(i, (i + step) % count) for i in range(count)])  15.9 us
    add x3, other arithmetic, shade(): colours[channel] + weight * palette[knot_index, channel][:, None, :]  2.65 us
    dot_general x1, matrix products, on_device(): jnp.dot(selector.reshape(-1, map_count), colormap.reshape(map_count, -1),...  1.37 us
    add x3, other arithmetic, shade(): colour[channel] = colour[channel] + weight_z * colours[channel][:, z]  1.33 us
    slice x1, local copies, waits for them, and re-layouts, on_device(): z_high = shift(mid[:, :, :1], 'gz', -1)  1.19 us
  transfers between devices with their start and end apart: 4, of which 0 were waited for; matrix products, arithmetic and copies ran while one was open for 7% of the time, Pallas kernels for 0%

commit v1 on v0

v1 whole, which is shorter than its diff:
```python
import functools

import jax
import jax.numpy as jnp
from jax import lax
from jax.experimental import pallas as pl
from jax.experimental.pallas import tpu as pltpu
from jax.sharding import PartitionSpec as P

LANES = 128
TILE = 8
CHUNK = 4


def shift(x, axis, step):
    count = lax.axis_size(axis)
    return lax.ppermute(x, axis, [(i, (i + step) % count) for i in range(count)])


def iota(shape, dim):
    return lax.broadcasted_iota(jnp.int32, shape, dim)


def gather(table, index):
    return jnp.take_along_axis(table, index, axis=1, mode="promise_in_bounds")


def edges_kernel(rate, v_ref, colormap_ref, pad_ref, zhi_ref, zlo_ref, xhi_ref, xlo_ref, table_ref, sem):
    planes, blocks = v_ref.shape[0], v_ref.shape[1]
    tall = planes // 3
    rows = tall // 2 - 2
    inner = pl.ds(1, blocks)
    copy = pltpu.make_async_copy(v_ref, pad_ref.at[:, inner], sem)
    copy.start()
    maps, knots = colormap_ref.shape[0], colormap_ref.shape[2]
    values = jnp.concatenate([colormap_ref[m] for m in range(maps)], axis=1)
    channel, lane = iota(values.shape, 0), iota(values.shape, 1)
    values = jnp.where(channel == 3, values * -rate, values)
    slopes = jnp.where(lane % knots == knots - 1, 0.0, pltpu.roll(values, LANES - 1, 1) - values)
    table_ref[...] = jnp.concatenate([values, slopes], axis=0)
    lane = iota((TILE, LANES), 1)
    flat = pad_ref.reshape(planes * (blocks + 2) * TILE, LANES)
    across = lambda plane, z: flat[pl.ds((plane * (blocks + 2) + 1) * TILE + z, blocks, stride=TILE), :]
    copy.wait()
    xhi = jnp.zeros((TILE, LANES), jnp.float32)
    xlo = jnp.zeros((TILE, LANES), jnp.float32)
    for c in range(3):
        for r in range(rows):
            k = c * rows + r
            first = c * tall + 2 * (r + 1)
            zlo_ref[k] = across(first, 0)
            zhi_ref[k] = across(first + 1, TILE - 1)
            for t in range(2):
                spot = 2 * k + t
                xhi = jnp.where(lane == spot, pltpu.roll(pad_ref[first + t, blocks], spot + 1, 1), xhi)
                xlo = jnp.where(lane == spot, pltpu.roll(pad_ref[first + t, 1], spot, 1), xlo)
    xhi_ref[...] = xhi
    xlo_ref[...] = xlo


def shade_kernel(knots, pad_in, zl_ref, zh_ref, xl_ref, xh_ref, table_ref, map_ref, out_ref, pad_ref, y_ref, t_ref):
    planes, blocks = pad_ref.shape[0], pad_ref.shape[1] - 2
    tall = planes // 3
    rows, depth = tall // 2 - 2, 2 * TILE
    terms = 4 * rows
    lane = iota((TILE, LANES), 1)
    tables = [jnp.broadcast_to(table_ref[k : k + 1, :], (TILE, LANES)) for k in range(8)]
    for k in range(6 * rows):
        plane = (k // (2 * rows)) * tall + 2 * ((k // 2) % rows + 1) + k % 2
        pad_ref[plane, 0] = pltpu.roll(xl_ref[...], LANES - 1 - k, 1)
        pad_ref[plane, blocks + 1] = pltpu.roll(xh_ref[...], (LANES - k) % LANES, 1)

    flat = pad_ref.reshape(planes * (blocks + 2) * TILE, LANES)

    def at(c, y, z, move=0):
        plane = c * tall + 2 * y + z // TILE
        return flat[pl.ds((plane * (blocks + 2) + 1 + move) * TILE + z % TILE, blocks, stride=TILE), :]

    def deep(c, r, z):
        if z < 0:
            return zl_ref[c * rows + r]
        if z == depth:
            return zh_ref[c * rows + r]
        return at(c, r + 1, z)

    last, first = lane == LANES - 1, lane == 0
    half = 0.5 * (knots - 1)
    for r in range(rows):
        offset = map_ref[r] * knots
        sums = [jnp.zeros((TILE, LANES), jnp.float32) for k in range(3)]
        log_light = jnp.zeros((TILE, LANES), jnp.float32)
        light = jnp.ones((TILE, LANES), jnp.float32)
        for start in range(0, depth, CHUNK):
            zs = range(start, start + CHUNK)
            dx, dy, dz = [], [], []
            for c in range(3):
                own = [at(c, r + 1, z) for z in zs]
                left = [jnp.where(last, at(c, r + 1, z, -1), u) for z, u in zip(zs, own)]
                right = [jnp.where(first, at(c, r + 1, z, 1), u) for z, u in zip(zs, own)]
                left = [pltpu.roll(u, 1, 1) for u in left]
                right = [pltpu.roll(u, LANES - 1, 1) for u in right]
                dx.append([b - a for a, b in zip(left, right)])
                dy.append([at(c, r + 2, z) - at(c, r, z) for z in zs])
                dz.append([deep(c, r, z + 1) - deep(c, r, z - 1) for z in zs])
            n = range(CHUNK)
            square = [dx[0][i] * dx[0][i] + dy[1][i] * dy[1][i] + dz[2][i] * dz[2][i] for i in n]
            cross = [dx[1][i] * dy[0][i] + dx[2][i] * dz[0][i] + dy[2][i] * dz[1][i] for i in n]
            total = [a + (b + b) for a, b in zip(square, cross)]
            position = [half + half * jnp.tanh(a * -0.0625) for a in total]
            knot = [a.astype(jnp.int32) for a in position]
            part = [a - k.astype(jnp.float32) for a, k in zip(position, knot)]
            index = [k + offset for k in knot]
            base = [[gather(tables[k], i) for k in range(4)] for i in index]
            slope = [[gather(tables[4 + k], i) for k in range(4)] for i in index]
            shades = [[b + p * s for b, s in zip(bs, ss)] for bs, ss, p in zip(base, slope, part)]
            for i in n:
                log_light = log_light + shades[i][3]
                behind = jnp.exp(log_light)
                weight = light - behind
                light = behind
                sums = [a + weight * s for a, s in zip(sums, shades[i])]
        for k, value in enumerate(sums + [log_light]):
            y_ref[:, k * rows + r, :] = value
    t_ref[...] = y_ref[...].reshape(LANES, LANES).T
    share = LANES // terms
    parts = [t_ref[pl.ds(j, terms, stride=share), :] for j in range(share)]
    group = iota((terms, LANES), 1) // terms
    bit = share // 2
    while bit:
        for j in range(share):
            if j & bit:
                continue
            one, two = parts[j], parts[j + bit]
            clear = (group & bit) == 0
            parts[j] = jnp.where(clear, one, pltpu.roll(two, bit * terms, 1))
            parts[j + bit] = jnp.where(clear, pltpu.roll(one, LANES - bit * terms, 1), two)
        bit //= 2
    for b in range(blocks):
        out_ref[b * terms : (b + 1) * terms, :] = parts[b]


def compose_kernel(seen_ref, out_ref):
    slabs = seen_ref.shape[0]
    rows = out_ref.shape[1]
    terms = 4 * rows
    share = out_ref.shape[2]
    lane, sub = iota((TILE, LANES), 1), iota((TILE, LANES), 0)
    term = lane % terms
    is_light = term >= 3 * rows
    ahead = jnp.zeros((TILE, LANES), jnp.float32)
    image = jnp.zeros((TILE, LANES), jnp.float32)
    for t in range(slabs // TILE):
        seen = seen_ref[t * TILE : (t + 1) * TILE, :]
        own = jnp.where(is_light, seen, 0.0)
        own = own + pltpu.roll(own, LANES - 2 * rows, 1)
        own = own + pltpu.roll(own, LANES - rows, 1)
        reached = own
        for step in (1, 2, 4):
            reached = reached + jnp.where(sub >= step, pltpu.roll(reached, step, 0), 0.0)
        image = image + jnp.exp(ahead + (reached - own)) * seen
        ahead = ahead + jnp.broadcast_to(reached[TILE - 1 :, :], (TILE, LANES))
    image = jnp.sum(image, axis=0, keepdims=True)
    image = jnp.where(is_light[:1], 1.0 - jnp.exp(ahead[:1]), image)
    image = jnp.broadcast_to(image, (terms, LANES))
    index = (iota((terms, LANES), 1) % share) * terms + iota((terms, LANES), 0)
    image = gather(image, index)
    for k in range(4):
        out_ref[k] = image[k * rows : (k + 1) * rows, :share]


def on_device(velocity, colormap, map_choice):
    slabs = lax.axis_size("gz")
    tall, depth, width = velocity.shape[1:]
    rows = tall - 2
    knots = colormap.shape[1]
    blocks = width // LANES
    planes = 3 * tall * depth // TILE
    rate = 4.0 / (depth * slabs)
    tiles = velocity.reshape(3 * tall, depth // TILE, TILE, blocks, LANES).transpose(0, 1, 3, 2, 4)
    tiles = pltpu.with_memory_space_constraint(tiles.reshape(planes, blocks, TILE, LANES), pltpu.HBM)
    whole = pl.BlockSpec(memory_space=pltpu.VMEM)
    params = pltpu.CompilerParams(vmem_limit_bytes=16 * 2**20)
    f32 = lambda *shape: jax.ShapeDtypeStruct(shape, jnp.float32)
    padded, z_last, z_first, x_last, x_first, table = pl.pallas_call(
        functools.partial(edges_kernel, rate),
        out_shape=(
            f32(planes, blocks + 2, TILE, LANES),
            f32(3 * rows, blocks, LANES),
            f32(3 * rows, blocks, LANES),
            f32(TILE, LANES),
            f32(TILE, LANES),
            f32(TILE, LANES),
        ),
        in_specs=[pl.BlockSpec(memory_space=pltpu.HBM), whole],
        out_specs=(whole,) * 6,
        scratch_shapes=[pltpu.SemaphoreType.DMA],
        compiler_params=params,
        name="edges",
    )(tiles, colormap.transpose(0, 2, 1))
    z_low = shift(z_last, "gz", 1)
    z_high = shift(z_first, "gz", -1)
    x_low = shift(x_last, "gx", 1)
    x_high = shift(x_first, "gx", -1)
    parts, _ = pl.pallas_call(
        functools.partial(shade_kernel, knots),
        out_shape=(f32(slabs, LANES), f32(*padded.shape)),
        in_specs=[whole] * 7,
        out_specs=(whole, whole),
        scratch_shapes=[pltpu.VMEM((blocks, 4 * rows, LANES), jnp.float32), pltpu.VMEM((LANES, LANES), jnp.float32)],
        input_output_aliases={0: 1},
        compiler_params=params,
        name="shade",
    )(padded, z_low, z_high, x_low, x_high, table, map_choice.reshape(rows, blocks, LANES))
    seen = lax.all_to_all(parts, "gz", 0, 0, tiled=True)
    return pl.pallas_call(
        compose_kernel,
        out_shape=f32(4, rows, width // slabs),
        in_specs=[whole],
        out_specs=whole,
        compiler_params=params,
        name="compose",
    )(seen)


def solution(mesh):
    placed = (P(None, None, "gz", "gx"), P(), P(None, "gx"))
    return jax.shard_map(
        on_device,
        mesh=mesh,
        in_specs=placed,
        out_specs=P(None, None, ("gx", "gz")),
        check_vma=False,
    )
```

time: 58.6 us -> 51.9 us (0.89)
  other arithmetic: 6.03 us -> 0 us
  Pallas kernels: 0 us -> 5.29 us
  local copies, waits for them, and re-layouts: 5.85 us -> 1.44 us
  matrix products: 1.37 us -> 0 us
  starting transfers between devices: 15.9 us -> 17.2 us
  blocking collectives: 28.5 us -> 27.5 us
    pallas_call x0 -> x3, Pallas kernels: none -> 5.29 us  [the longest x1 3.01 us: on_device(): pl.pallas_call(functools.partial(shade_kernel, knots), out_shape=(f32(sla...]
    add x6 -> x0, other arithmetic: 3.98 us -> none  [the longest x3 2.65 us: shade(): colours[channel] + weight * palette[knot_index, channel][:, None, :]]
    slice x6 -> x0, local copies, waits for them, and re-layouts: 3.17 us -> none  [the longest x1 1.19 us: on_device(): z_high = shift(mid[:, :, :1], 'gz', -1)]
    dot_general x1 -> x0, matrix products: 1.37 us -> none  [on_device(): jnp.dot(selector.reshape(-1, map_count), colormap.reshape(map_count, -1),...]
    reshape x2 -> x0, local copies, waits for them, and re-layouts: 1.27 us -> none  [the longest x1 0.68 us: on_device(): return image.reshape(channels, rows, share)]
    ppermute x4, starting transfers between devices: 15.9 us -> 17.2 us  [shift(): lax.ppermute(x, axis, [(i, (i + step) % count) for i in range(count)])]
    all_to_all x1, blocking collectives: 28.5 us -> 27.5 us  [on_device(): seen = lax.all_to_all(parts, 'gz', 0, 0, tiled=True)]
    mul x3 -> x0, other arithmetic: 0.85 us -> none  [the longest x1 0.67 us: shade(): along_x = (in_x[..., 2:] - in_x[..., :-2]) * 0.5]
  transfers between devices with their start and end apart: 4 -> 4, of which waited for: 0 -> 0; matrix products, arithmetic and copies ran while one was open for 7% -> 1% of each run, Pallas kernels for 0% -> 0%
where the time goes in v1:
time: 51.9 us; the launch traced here: 51.5 us
  blocking collectives  27.5 us (53%)
  starting transfers between devices  17.2 us (33%)
  Pallas kernels  5.29 us (10%)
  local copies, waits for them, and re-layouts  1.44 us (3%)
    all_to_all x1, blocking collectives, on_device(): seen = lax.all_to_all(parts, 'gz', 0, 0, tiled=True)  27.5 us
    ppermute x4, starting transfers between devices, shift(): lax.ppermute(x, axis, [(i, (i + step) % count) for i in range(count)])  17.2 us
    pallas_call x1, Pallas kernels, on_device(): pl.pallas_call(functools.partial(shade_kernel, knots), out_shape=(f32(sla...  3.01 us
    unnamed x3, local copies, waits for them, and re-layouts  1.44 us
    pallas_call x1, Pallas kernels, on_device(): pl.pallas_call(functools.partial(edges_kernel, rate), out_shape=(f32(plan...  1.42 us
  transfers between devices with their start and end apart: 4, of which 0 were waited for; matrix products, arithmetic and copies ran while one was open for 1% of the time, Pallas kernels for 0%

profile of v1, /device:TPU:1, one launch (start us, length us, event | category | flops | bytes accessed | tf_op | source)
XLA Modules:
  0.0 51.5 jit_solution(18068919074146675845)
XLA Ops:
  0.0 0.0 copy-start
  0.0 0.7 %copy-done = f32[8,16,4]{1,2,0:T(4,128)S(1)} copy-done((f32[8,16,4]{1,2,0:T(4,128)S(1)}, f32[8,16,4]{1,2,0:T(4,128)}, u32[]{:S(2)}) %copy-start) | copy-done | bytes 2072
  0.7 1.4 %edges.1 = (f32[36,10,8,128]{3,2,1,0:T(8,128)S(1)}, f32[12,8,128]{2,1,0:T(8,128)S(1)}, f32[12,8,128]{2,1,0:T(8,128)S(1)}, f32[8,128]{1,0:T(8,128)S(1)}, f32[8,128]{1,0:T(8,128)S(1)}, /*index=5*/f32[8,128]{1,0:T(8,128)S(1)}) custom-call(f32[36,8,8,128]{3,2,1,0:T(8,128)} %bitcast.18, f32[8,4,16]{2,1,0:T(4,128)S(1)} %bitcast.17), custom_call_target="tpu_custom_call" | custom-call | tf_op jit(solution)/shard_map/edges/pallas_call | solution.py:184
  2.1 5.4 %collective-permute-start = (f32[12,8,128]{2,1,0:T(8,128)S(1)}, f32[12,8,128]{2,1,0:T(8,128)S(1)}, u32[]{:S(2)}, u32[]{:S(2)}) collective-permute-start(f32[12,8,128]{2,1,0:T(8,128)S(1)} %get-tuple-element.13), channel_id=1, source_target_pairs={{0,4},{4,8},{8,12},{12,16},{16,20},{20,24},{24,28},{28,32},{32,36}... | collective-permute-start | bytes 147464 | tf_op jit(solution)/shard_map/ppermute | solution.py:17
  7.5 5.3 %collective-permute-start.1 = (f32[12,8,128]{2,1,0:T(8,128)S(1)}, f32[12,8,128]{2,1,0:T(8,128)S(1)}, u32[]{:S(2)}, u32[]{:S(2)}) collective-permute-start(f32[12,8,128]{2,1,0:T(8,128)S(1)} %get-tuple-element.14), channel_id=1, source_target_pairs={{0,508},{4,0},{8,4},{12,8},{16,12},{20,16},{24,20},{28,24},{32,28}... | collective-permute-start | bytes 147464 | tf_op jit(solution)/shard_map/ppermute | solution.py:17
  12.8 1.9 %collective-permute-start.2 = (f32[8,128]{1,0:T(8,128)S(1)}, f32[8,128]{1,0:T(8,128)S(1)}, u32[]{:S(2)}, u32[]{:S(2)}) collective-permute-start(f32[8,128]{1,0:T(8,128)S(1)} %get-tuple-element.15), channel_id=1, source_target_pairs={{0,1},{1,2},{2,3},{3,0},{4,5},{5,6},{6,7},{7,4},{8,9},{9,10},{10,1... | collective-permute-start | bytes 12296 | tf_op jit(solution)/shard_map/ppermute | solution.py:17
  14.8 4.6 %collective-permute-start.3 = (f32[8,128]{1,0:T(8,128)S(1)}, f32[8,128]{1,0:T(8,128)S(1)}, u32[]{:S(2)}, u32[]{:S(2)}) collective-permute-start(f32[8,128]{1,0:T(8,128)S(1)} %get-tuple-element.16), channel_id=1, source_target_pairs={{0,3},{1,0},{2,1},{3,2},{4,7},{5,4},{6,5},{7,6},{8,11},{9,8},{10,9... | collective-permute-start | bytes 12296 | tf_op jit(solution)/shard_map/ppermute | solution.py:17
  19.3 0.7 %copy.8 = s32[1,4,8,128]{3,2,1,0:T(8,128)S(1)} copy(s32[1,4,8,128]{3,1,2,0:T(4,128)} %bitcast.19) | data formatting | bytes 32768
  20.1 0.0 collective-permute-done.2.xl_ref
  20.1 0.0 collective-permute-done.3.xh_ref
  20.1 0.0 collective-permute-done.zl_ref
  20.1 0.0 collective-permute-done.1.zh_ref
  20.1 3.0 %shade.1 = (f32[128,128]{1,0:T(8,128)S(1)}, f32[36,10,8,128]{3,2,1,0:T(8,128)S(1)}) custom-call(f32[36,10,8,128]{3,2,1,0:T(8,128)S(1)} %get-tuple-element.12.pad_in, f32[12,8,128]{2,1,0:T(8,128)S(1)} %collective-permute-done.zl_ref, f32[12,8,128]{2,1,0:T(8,128)S(1)} %collective-permute-done.1.zh_ref, ...), custom_call_target="tpu_custom_call", output_to_operand_aliasing={{1}: (0, {})} | custom-call | tf_op jit(solution)/shard_map/shade/pallas_call | solution.py:204
  23.1 27.5 %all_to_all.11 = f32[128,1,128]{2,1,0:T(1,128)S(1)} all-to-all(f32[128,1,128]{2,1,0:T(1,128)S(1)} %bitcast.16), channel_id=1, replica_groups=mesh['gz'=128,'gx'=4] {'gz'}, dimensions={0} | all-to-all | bytes 131072 | tf_op jit(solution)/shard_map/all_to_all | solution.py:214
  50.6 0.9 %compose.1 = f32[4,4,8]{2,1,0:T(4,128)} custom-call(f32[128,128]{1,0:T(8,128)S(1)} %bitcast.14), custom_call_target="tpu_custom_call" | custom-call | tf_op jit(solution)/shard_map/compose/pallas_call | solution.py:215
Async XLA Ops:
  0.0 0.7 %copy-start = (f32[8,16,4]{1,2,0:T(4,128)S(1)}, f32[8,16,4]{1,2,0:T(4,128)}, u32[]{:S(2)}) copy-start(f32[8,16,4]{1,2,0:T(4,128)} %param.4) | copy-start | bytes 6148
  2.1 17.9 %collective-permute-start = (f32[12,8,128]{2,1,0:T(8,128)S(1)}, f32[12,8,128]{2,1,0:T(8,128)S(1)}, u32[]{:S(2)}, u32[]{:S(2)}) collective-permute-start(f32[12,8,128]{2,1,0:T(8,128)S(1)} %get-tuple-element.13), channel_id=1, source_target_pairs={{0,4},{4,8},{8,12},{12,16},{16,20},{20,24},{24,28},{28,32},{32,36}... | collective-permute-start | bytes 147464 | tf_op jit(solution)/shard_map/ppermute | solution.py:17
  7.5 12.5 %collective-permute-start.1 = (f32[12,8,128]{2,1,0:T(8,128)S(1)}, f32[12,8,128]{2,1,0:T(8,128)S(1)}, u32[]{:S(2)}, u32[]{:S(2)}) collective-permute-start(f32[12,8,128]{2,1,0:T(8,128)S(1)} %get-tuple-element.14), channel_id=1, source_target_pairs={{0,508},{4,0},{8,4},{12,8},{16,12},{20,16},{24,20},{28,24},{32,28}... | collective-permute-start | bytes 147464 | tf_op jit(solution)/shard_map/ppermute | solution.py:17
  12.8 7.2 %collective-permute-start.2 = (f32[8,128]{1,0:T(8,128)S(1)}, f32[8,128]{1,0:T(8,128)S(1)}, u32[]{:S(2)}, u32[]{:S(2)}) collective-permute-start(f32[8,128]{1,0:T(8,128)S(1)} %get-tuple-element.15), channel_id=1, source_target_pairs={{0,1},{1,2},{2,3},{3,0},{4,5},{5,6},{6,7},{7,4},{8,9},{9,10},{10,1... | collective-permute-start | bytes 12296 | tf_op jit(solution)/shard_map/ppermute | solution.py:17
  14.8 5.3 %collective-permute-start.3 = (f32[8,128]{1,0:T(8,128)S(1)}, f32[8,128]{1,0:T(8,128)S(1)}, u32[]{:S(2)}, u32[]{:S(2)}) collective-permute-start(f32[8,128]{1,0:T(8,128)S(1)} %get-tuple-element.16), channel_id=1, source_target_pairs={{0,3},{1,0},{2,1},{3,2},{4,7},{5,4},{6,5},{7,6},{8,11},{9,8},{10,9... | collective-permute-start | bytes 12296 | tf_op jit(solution)/shard_map/ppermute | solution.py:17

commit v2 on v1

v2 whole, which is shorter than its diff:
```python
import functools

import jax
import jax.numpy as jnp
from jax import lax
from jax.experimental import pallas as pl
from jax.experimental.pallas import tpu as pltpu
from jax.sharding import PartitionSpec as P


LANES = 128
TILE = 8
CHUNK = 4


def swap(x, axis, first):
    count = lax.axis_size(axis)
    pairs = [(i % count, (i + 1) % count) for i in range(first, count + first, 2)]
    return lax.ppermute(x, axis, pairs + [(b, a) for a, b in pairs])


def iota(shape, dim):
    return lax.broadcasted_iota(jnp.int32, shape, dim)


def gather(table, index):
    return jnp.take_along_axis(table, index, axis=1, mode="promise_in_bounds")


LEAD, PITCH = 8, 24


def edges_kernel(rate, v_ref, colormap_hbm, map_hbm, pad_ref, z0_ref, z1_ref, x0_ref, x1_ref, table_ref, map_ref, colormap_ref, sem, small):
    planes, blocks = v_ref.shape[0], v_ref.shape[1]
    tall = planes // 6
    rows, depth = tall - 2, 2 * TILE
    copies = [pltpu.make_async_copy(v_ref.at[:, b], pad_ref.at[:, :, LEAD + b, :], sem.at[b]) for b in range(blocks)]
    for copy in copies:
        copy.start()
    few = [
        pltpu.make_async_copy(colormap_hbm, colormap_ref, small.at[0]),
        pltpu.make_async_copy(map_hbm, map_ref, small.at[1]),
    ]
    for copy in few:
        copy.start()
    few[0].wait()
    maps, knots = colormap_ref.shape[0], colormap_ref.shape[2]
    values = jnp.concatenate([colormap_ref[m] for m in range(maps)], axis=1)
    channel, lane = iota(values.shape, 0), iota(values.shape, 1)
    values = jnp.where(channel == 3, values * -rate, values)
    slopes = jnp.where(lane % knots == knots - 1, 0.0, pltpu.roll(values, LANES - 1, 1) - values)
    table_ref[...] = jnp.concatenate([values, slopes], axis=0)
    few[1].wait()
    lane = iota((TILE, LANES), 1)
    flat = pad_ref.reshape(planes * TILE * PITCH, LANES)
    z_even, x_even = lax.axis_index("gz") % 2 == 0, lax.axis_index("gx") % 2 == 0
    for copy in copies:
        copy.wait()
    xhi = jnp.zeros((TILE, LANES), jnp.float32)
    xlo = jnp.zeros((TILE, LANES), jnp.float32)
    for c in range(3):
        for r in range(rows):
            k = c * rows + r
            first = (c * tall + r + 1) * depth * PITCH + LEAD
            zlo = flat[pl.ds(first, blocks), :]
            zhi = flat[pl.ds(first + (depth - 1) * PITCH, blocks), :]
            z0_ref[k] = jnp.where(z_even, zhi, zlo)
            z1_ref[k] = jnp.where(z_even, zlo, zhi)
            for t in range(2):
                spot = 2 * k + t
                start = first + t * TILE * PITCH
                ends = flat[pl.ds(start + blocks - 1, TILE, stride=PITCH), :]
                xhi = jnp.where(lane == spot, pltpu.roll(ends, spot + 1, 1), xhi)
                ends = flat[pl.ds(start, TILE, stride=PITCH), :]
                xlo = jnp.where(lane == spot, pltpu.roll(ends, spot, 1), xlo)
    x0_ref[...] = jnp.where(x_even, xhi, xlo)
    x1_ref[...] = jnp.where(x_even, xlo, xhi)


def shade_kernel(knots, pad_in, z0_ref, z1_ref, x0_ref, x1_ref, table_ref, map_ref, out_ref, pad_ref, y_ref, t_ref, index_ref, part_ref):
    blocks = TILE
    tall = pad_ref.shape[0] // 6
    rows, depth = tall - 2, 2 * TILE
    terms = 4 * rows
    lane = iota((TILE, LANES), 1)
    flat = pad_ref.reshape(pad_ref.shape[0] * TILE * PITCH, LANES)
    tables = [jnp.broadcast_to(table_ref[k : k + 1, :], (TILE, LANES)) for k in range(8)]
    z_even, x_even = lax.axis_index("gz") % 2 == 0, lax.axis_index("gx") % 2 == 0
    xl = jnp.where(x_even, x1_ref[...], x0_ref[...])
    xh = jnp.where(x_even, x0_ref[...], x1_ref[...])
    for k in range(6 * rows):
        start = ((k // (2 * rows)) * tall + (k // 2) % rows + 1) * depth * PITCH + (k % 2) * TILE * PITCH + LEAD
        flat[pl.ds(start - 1, TILE, stride=PITCH), :] = pltpu.roll(xl, LANES - 1 - k, 1)
        flat[pl.ds(start + blocks, TILE, stride=PITCH), :] = pltpu.roll(xh, (LANES - k) % LANES, 1)

    def at(c, y, z, move=0):
        return flat[pl.ds(((c * tall + y) * depth + z) * PITCH + LEAD + move, blocks), :]

    def deep(c, r, z):
        if z < 0:
            return jnp.where(z_even, z1_ref[c * rows + r], z0_ref[c * rows + r])
        if z == depth:
            return jnp.where(z_even, z0_ref[c * rows + r], z1_ref[c * rows + r])
        return at(c, r + 1, z)

    last, first = lane == LANES - 1, lane == 0
    half = 0.5 * (knots - 1)

    def locate(r, zs):
        dx, dy, dz = [], [], []
        for c in range(3):
            own = [at(c, r + 1, z) for z in zs]
            left = [jnp.where(last, at(c, r + 1, z, -1), u) for z, u in zip(zs, own)]
            right = [jnp.where(first, at(c, r + 1, z, 1), u) for z, u in zip(zs, own)]
            left = [pltpu.roll(u, 1, 1) for u in left]
            right = [pltpu.roll(u, LANES - 1, 1) for u in right]
            dx.append([b - a for a, b in zip(left, right)])
            dy.append([at(c, r + 2, z) - at(c, r, z) for z in zs])
            dz.append([deep(c, r, z + 1) - deep(c, r, z - 1) for z in zs])
        n = range(len(zs))
        square = [dx[0][i] * dx[0][i] + dy[1][i] * dy[1][i] + dz[2][i] * dz[2][i] for i in n]
        cross = [dx[1][i] * dy[0][i] + dx[2][i] * dz[0][i] + dy[2][i] * dz[1][i] for i in n]
        total = [a + (b + b) for a, b in zip(square, cross)]
        position = [half + half * jnp.tanh(a * -0.0625) for a in total]
        knot = [a.astype(jnp.int32) for a in position]
        offset = map_ref[pl.ds(r, blocks, stride=rows), :] * knots
        for z, p, k in zip(zs, position, knot):
            part_ref[r, z] = p - k.astype(jnp.float32)
            index_ref[r, z] = k + offset

    def paint(r, zs, state):
        sums, log_light, light = state
        index = [index_ref[r, z] for z in zs]
        part = [part_ref[r, z] for z in zs]
        base = [[gather(tables[k], i) for k in range(4)] for i in index]
        slope = [[gather(tables[4 + k], i) for k in range(4)] for i in index]
        shades = [[b + p * s for b, s in zip(bs, ss)] for bs, ss, p in zip(base, slope, part)]
        for here in shades:
            log_light = log_light + here[3]
            behind = jnp.exp(log_light)
            weight = light - behind
            light = behind
            sums = [a + weight * s for a, s in zip(sums, here)]
        return sums, log_light, light

    zero = jnp.zeros((TILE, LANES), jnp.float32)
    chunks = [range(start, start + CHUNK) for start in range(0, depth, CHUNK)]
    for r in range(rows + 1):
        state = [zero, zero, zero], zero, jnp.ones((TILE, LANES), jnp.float32)
        for zs in chunks:
            if r < rows:
                locate(r, zs)
            if r:
                state = paint(r - 1, zs, state)
        if r:
            for k, value in enumerate(state[0] + [state[1]]):
                y_ref[pl.ds(k * rows + r - 1, blocks, stride=terms), :] = value
    t_ref[...] = y_ref[...].T
    share = LANES // terms
    parts = [t_ref[pl.ds(j, terms, stride=share), :] for j in range(share)]
    group = iota((terms, LANES), 1) // terms
    bit = share // 2
    while bit:
        for j in range(share):
            if j & bit:
                continue
            one, two = parts[j], parts[j + bit]
            clear = (group & bit) == 0
            parts[j] = jnp.where(clear, one, pltpu.roll(two, bit * terms, 1))
            parts[j + bit] = jnp.where(clear, pltpu.roll(one, LANES - bit * terms, 1), two)
        bit //= 2
    for b in range(blocks):
        out_ref[b * terms : (b + 1) * terms, :] = parts[b]


def compose_kernel(seen_ref, out_ref):
    slabs = seen_ref.shape[0]
    rows = out_ref.shape[1]
    terms = 4 * rows
    share = out_ref.shape[2]
    lane, sub = iota((TILE, LANES), 1), iota((TILE, LANES), 0)
    term = lane % terms
    is_light = term >= 3 * rows
    ahead = jnp.zeros((TILE, LANES), jnp.float32)
    image = jnp.zeros((TILE, LANES), jnp.float32)
    for t in range(slabs // TILE):
        seen = seen_ref[t * TILE : (t + 1) * TILE, :]
        own = jnp.where(is_light, seen, 0.0)
        own = own + pltpu.roll(own, LANES - 2 * rows, 1)
        own = own + pltpu.roll(own, LANES - rows, 1)
        reached = own
        for step in (1, 2, 4):
            reached = reached + jnp.where(sub >= step, pltpu.roll(reached, step, 0), 0.0)
        image = image + jnp.exp(ahead + (reached - own)) * seen
        ahead = ahead + jnp.broadcast_to(reached[TILE - 1 :, :], (TILE, LANES))
    image = jnp.sum(image, axis=0, keepdims=True)
    image = jnp.where(is_light[:1], 1.0 - jnp.exp(ahead[:1]), image)
    image = jnp.broadcast_to(image, (terms, LANES))
    index = (iota((terms, LANES), 1) % share) * terms + iota((terms, LANES), 0)
    image = gather(image, index)
    for k in range(4):
        out_ref[k] = image[k * rows : (k + 1) * rows, :share]


def on_device(velocity, colormap, map_choice):
    slabs = lax.axis_size("gz")
    tall, depth, width = velocity.shape[1:]
    rows = tall - 2
    knots = colormap.shape[1]
    blocks = width // LANES
    planes = 3 * tall * depth // TILE
    rate = 4.0 / (depth * slabs)
    tiles = velocity.reshape(3 * tall, depth // TILE, TILE, blocks, LANES).transpose(0, 1, 3, 2, 4)
    tiles = tiles.reshape(planes, blocks, TILE, LANES)
    choice = map_choice.reshape(rows, blocks, LANES).transpose(1, 0, 2).reshape(blocks * rows, LANES)
    hbm = lambda x: pltpu.with_memory_space_constraint(x, pltpu.HBM)
    whole = pl.BlockSpec(memory_space=pltpu.VMEM)
    params = pltpu.CompilerParams(vmem_limit_bytes=16 * 2**20)
    f32 = lambda *shape: jax.ShapeDtypeStruct(shape, jnp.float32)
    padded, z0, z1, x0, x1, table, choice = pl.pallas_call(
        functools.partial(edges_kernel, rate),
        out_shape=(
            f32(planes, TILE, PITCH, LANES),
            f32(3 * rows, blocks, LANES),
            f32(3 * rows, blocks, LANES),
            f32(TILE, LANES),
            f32(TILE, LANES),
            f32(TILE, LANES),
            jax.ShapeDtypeStruct(choice.shape, jnp.int32),
        ),
        in_specs=[pl.BlockSpec(memory_space=pltpu.HBM)] * 3,
        out_specs=(whole,) * 7,
        scratch_shapes=[
            pltpu.VMEM((colormap.shape[0], 4, knots), jnp.float32),
            pltpu.SemaphoreType.DMA((blocks,)),
            pltpu.SemaphoreType.DMA((2,)),
        ],
        compiler_params=params,
        name="edges",
    )(hbm(tiles), hbm(colormap.transpose(0, 2, 1)), hbm(choice))
    x0 = swap(x0, "gx", 0)
    x1 = swap(x1, "gx", 1)
    z1 = swap(z1, "gz", 1)
    z0 = swap(z0, "gz", 0)
    parts, _ = pl.pallas_call(
        functools.partial(shade_kernel, knots),
        out_shape=(f32(slabs, LANES), f32(*padded.shape)),
        in_specs=[whole] * 7,
        out_specs=(whole, whole),
        scratch_shapes=[
            pltpu.VMEM((LANES, LANES), jnp.float32),
            pltpu.VMEM((LANES, LANES), jnp.float32),
            pltpu.VMEM((rows, depth, TILE, LANES), jnp.int32),
            pltpu.VMEM((rows, depth, TILE, LANES), jnp.float32),
        ],
        input_output_aliases={0: 1},
        compiler_params=params,
        name="shade",
    )(padded, z0, z1, x0, x1, table, choice)
    seen = lax.all_to_all(parts, "gz", 0, 0, tiled=True)
    return pl.pallas_call(
        compose_kernel,
        out_shape=f32(4, rows, width // slabs),
        in_specs=[whole],
        out_specs=whole,
        compiler_params=params,
        name="compose",
    )(seen)


def solution(mesh):
    placed = (P(None, None, "gz", "gx"), P(), P(None, "gx"))
    return jax.shard_map(
        on_device,
        mesh=mesh,
        in_specs=placed,
        out_specs=P(None, None, ("gx", "gz")),
        check_vma=False,
    )
```

time: 51.9 us -> 49.1 us (0.946)
  waiting for transfers between devices: 0.02 us -> 3.93 us
  starting transfers between devices: 17.2 us -> 14.5 us
  blocking collectives: 27.5 us -> 26 us
  local copies, waits for them, and re-layouts: 1.44 us -> 0 us
  Pallas kernels: 5.29 us -> 4.37 us
    ppermute x4, waiting for transfers between devices: 0.02 us -> 3.93 us  [swap(): return lax.ppermute(x, axis, pairs + [(b, a) for a, b in pairs])]
    ppermute x4, starting transfers between devices: 17.2 us -> 14.5 us  [swap(): return lax.ppermute(x, axis, pairs + [(b, a) for a, b in pairs])]
    all_to_all x1, blocking collectives: 27.5 us -> 26 us  [on_device(): seen = lax.all_to_all(parts, 'gz', 0, 0, tiled=True)]
    unnamed x3 -> x0, local copies, waits for them, and re-layouts: 1.44 us -> none
    pallas_call x1, Pallas kernels: 3.01 us -> 1.93 us  [on_device(): pl.pallas_call(functools.partial(shade_kernel, knots), out_shape=(f32(sla...]
  transfers between devices with their start and end apart: 4 -> 4, of which waited for: 0 -> 2; matrix products, arithmetic and copies ran while one was open for 1% -> 0% of each run, Pallas kernels for 0% -> 0%
where the time goes in v2:
time: 49.1 us; the launch traced here: 48.8 us
  blocking collectives  26 us (53%)
  starting transfers between devices  14.5 us (30%)
  Pallas kernels  4.37 us (9%)
  waiting for transfers between devices  3.93 us (8%)
    all_to_all x1, blocking collectives, on_device(): seen = lax.all_to_all(parts, 'gz', 0, 0, tiled=True)  26 us
    ppermute x4, starting transfers between devices, swap(): return lax.ppermute(x, axis, pairs + [(b, a) for a, b in pairs])  14.5 us
    ppermute x4, waiting for transfers between devices, swap(): return lax.ppermute(x, axis, pairs + [(b, a) for a, b in pairs])  3.93 us
    pallas_call x1, Pallas kernels, on_device(): pl.pallas_call(functools.partial(shade_kernel, knots), out_shape=(f32(sla...  1.93 us
    pallas_call x1, Pallas kernels, on_device(): pl.pallas_call(functools.partial(edges_kernel, rate), out_shape=(f32(plan...  1.57 us
  transfers between devices with their start and end apart: 4, of which 2 were waited for; matrix products, arithmetic and copies ran while one was open for 0% of the time, Pallas kernels for 0%

profile of v2, /device:TPU:1, one launch (start us, length us, event | category | flops | bytes accessed | tf_op | source)
XLA Modules:
  0.0 48.8 jit_solution(7091114350573910338)
XLA Ops:
  0.0 1.6 %edges.1 = (f32[36,8,24,128]{3,2,1,0:T(8,128)S(1)}, f32[12,8,128]{2,1,0:T(8,128)S(1)}, f32[12,8,128]{2,1,0:T(8,128)S(1)}, f32[8,128]{1,0:T(8,128)S(1)}, f32[8,12...) custom-call(f32[36,8,8,128]{3,2,1,0:T(8,128)} %bitcast.17, f32[8,4,16]{2,1,0:T(4,128)} %bitcast.18, ...), custom_call_target="tpu_custom_call" | custom-call | tf_op jit(solution)/shard_map/edges/pallas_call | solution.py:220
  1.6 8.7 %collective-permute-start = (f32[12,8,128]{2,1,0:T(8,128)S(1)}, f32[12,8,128]{2,1,0:T(8,128)S(1)}, u32[]{:S(2)}, u32[]{:S(2)}) collective-permute-start(f32[12,8,128]{2,1,0:T(8,128)S(1)} %get-tuple-element.14), channel_id=1, source_target_pairs={{0,4},{8,12},{16,20},{24,28},{32,36},{40,44},{48,52},{56,60},{64,6... | collective-permute-start | bytes 147464 | tf_op jit(solution)/shard_map/ppermute | solution.py:19
  10.3 1.9 %collective-permute-start.1 = (f32[12,8,128]{2,1,0:T(8,128)S(1)}, f32[12,8,128]{2,1,0:T(8,128)S(1)}, u32[]{:S(2)}, u32[]{:S(2)}) collective-permute-start(f32[12,8,128]{2,1,0:T(8,128)S(1)} %get-tuple-element.15), channel_id=1, source_target_pairs={{4,8},{12,16},{20,24},{28,32},{36,40},{44,48},{52,56},{60,64},{68,... | collective-permute-start | bytes 147464 | tf_op jit(solution)/shard_map/ppermute | solution.py:19
  12.3 1.9 %collective-permute-start.2 = (f32[8,128]{1,0:T(8,128)S(1)}, f32[8,128]{1,0:T(8,128)S(1)}, u32[]{:S(2)}, u32[]{:S(2)}) collective-permute-start(f32[8,128]{1,0:T(8,128)S(1)} %get-tuple-element.16), channel_id=1, source_target_pairs={{0,1},{2,3},{1,0},{3,2},{4,5},{6,7},{5,4},{7,6},{8,9},{10,11},{9,8... | collective-permute-start | bytes 12296 | tf_op jit(solution)/shard_map/ppermute | solution.py:19
  14.2 1.9 %collective-permute-start.3 = (f32[8,128]{1,0:T(8,128)S(1)}, f32[8,128]{1,0:T(8,128)S(1)}, u32[]{:S(2)}, u32[]{:S(2)}) collective-permute-start(f32[8,128]{1,0:T(8,128)S(1)} %get-tuple-element.17), channel_id=1, source_target_pairs={{1,2},{3,0},{2,1},{0,3},{5,6},{7,4},{6,5},{4,7},{9,10},{11,8},{10,... | collective-permute-start | bytes 12296 | tf_op jit(solution)/shard_map/ppermute | solution.py:19
  16.1 0.5 %collective-permute-done.2.x0_ref = f32[8,128]{1,0:T(8,128)S(1)} collective-permute-done((f32[8,128]{1,0:T(8,128)S(1)}, f32[8,128]{1,0:T(8,128)S(1)}, u32[]{:S(2)}, u32[]{:S(2)}) %collective-permute-start.2) | collective-permute-done | bytes 4128 | tf_op jit(solution)/shard_map/ppermute | solution.py:19
  16.6 3.4 %collective-permute-done.3.x1_ref = f32[8,128]{1,0:T(8,128)S(1)} collective-permute-done((f32[8,128]{1,0:T(8,128)S(1)}, f32[8,128]{1,0:T(8,128)S(1)}, u32[]{:S(2)}, u32[]{:S(2)}) %collective-permute-start.3) | collective-permute-done | bytes 4128 | tf_op jit(solution)/shard_map/ppermute | solution.py:19
  20.1 0.0 collective-permute-done.z0_ref
  20.1 0.0 collective-permute-done.1.z1_ref
  20.1 1.9 %shade.1 = (f32[128,128]{1,0:T(8,128)S(1)}, f32[36,8,24,128]{3,2,1,0:T(8,128)S(1)}) custom-call(f32[36,8,24,128]{3,2,1,0:T(8,128)S(1)} %get-tuple-element.13.pad_in, f32[12,8,128]{2,1,0:T(8,128)S(1)} %collective-permute-done.z0_ref, f32[12,8,128]{2,1,0:T(8,128)S(1)} %collective-permute-done.1.z1_ref, ...), custom_call_target="tpu_custom_call", output_to_operand_aliasing={{1}: (0, {})} | custom-call | tf_op jit(solution)/shard_map/shade/pallas_call | solution.py:245
  22.0 26.0 %all_to_all.11 = f32[128,1,128]{2,1,0:T(1,128)S(1)} all-to-all(f32[128,1,128]{2,1,0:T(1,128)S(1)} %bitcast.16), channel_id=1, replica_groups=mesh['gz'=128,'gx'=4] {'gz'}, dimensions={0} | all-to-all | bytes 131072 | tf_op jit(solution)/shard_map/all_to_all | solution.py:260
  47.9 0.9 %compose.1 = f32[4,4,8]{2,1,0:T(4,128)} custom-call(f32[128,128]{1,0:T(8,128)S(1)} %bitcast.15), custom_call_target="tpu_custom_call" | custom-call | tf_op jit(solution)/shard_map/compose/pallas_call | solution.py:261
Async XLA Ops:
  1.6 18.5 %collective-permute-start = (f32[12,8,128]{2,1,0:T(8,128)S(1)}, f32[12,8,128]{2,1,0:T(8,128)S(1)}, u32[]{:S(2)}, u32[]{:S(2)}) collective-permute-start(f32[12,8,128]{2,1,0:T(8,128)S(1)} %get-tuple-element.14), channel_id=1, source_target_pairs={{0,4},{8,12},{16,20},{24,28},{32,36},{40,44},{48,52},{56,60},{64,6... | collective-permute-start | bytes 147464 | tf_op jit(solution)/shard_map/ppermute | solution.py:19
  10.3 9.7 %collective-permute-start.1 = (f32[12,8,128]{2,1,0:T(8,128)S(1)}, f32[12,8,128]{2,1,0:T(8,128)S(1)}, u32[]{:S(2)}, u32[]{:S(2)}) collective-permute-start(f32[12,8,128]{2,1,0:T(8,128)S(1)} %get-tuple-element.15), channel_id=1, source_target_pairs={{4,8},{12,16},{20,24},{28,32},{36,40},{44,48},{52,56},{60,64},{68,... | collective-permute-start | bytes 147464 | tf_op jit(solution)/shard_map/ppermute | solution.py:19
  12.3 4.4 %collective-permute-start.2 = (f32[8,128]{1,0:T(8,128)S(1)}, f32[8,128]{1,0:T(8,128)S(1)}, u32[]{:S(2)}, u32[]{:S(2)}) collective-permute-start(f32[8,128]{1,0:T(8,128)S(1)} %get-tuple-element.16), channel_id=1, source_target_pairs={{0,1},{2,3},{1,0},{3,2},{4,5},{6,7},{5,4},{7,6},{8,9},{10,11},{9,8... | collective-permute-start | bytes 12296 | tf_op jit(solution)/shard_map/ppermute | solution.py:19
  14.2 5.9 %collective-permute-start.3 = (f32[8,128]{1,0:T(8,128)S(1)}, f32[8,128]{1,0:T(8,128)S(1)}, u32[]{:S(2)}, u32[]{:S(2)}) collective-permute-start(f32[8,128]{1,0:T(8,128)S(1)} %get-tuple-element.17), channel_id=1, source_target_pairs={{1,2},{3,0},{2,1},{0,3},{5,6},{7,4},{6,5},{4,7},{9,10},{11,8},{10,... | collective-permute-start | bytes 12296 | tf_op jit(solution)/shard_map/ppermute | solution.py:19

commit v3 on v2

v3 whole, which is shorter than its diff:
```python
import functools

import jax
import jax.numpy as jnp
from jax import lax
from jax.experimental import pallas as pl
from jax.experimental.pallas import tpu as pltpu
from jax.sharding import PartitionSpec as P


LANES = 128
TILE = 8
CHUNK = 4


def swap(x, axis, first):
    count = lax.axis_size(axis)
    pairs = [(i % count, (i + 1) % count) for i in range(first, count + first, 2)]
    return lax.ppermute(x, axis, pairs + [(b, a) for a, b in pairs])


def iota(shape, dim):
    return lax.broadcasted_iota(jnp.int32, shape, dim)


def gather(table, index):
    return jnp.take_along_axis(table, index, axis=1, mode="promise_in_bounds")


LEAD, PITCH = 8, 24


def edges_kernel(v_ref, z0_ref, z1_ref, x_out_ref, z_ref, x_ref, z_sem, x_sem):
    tall, blocks = v_ref.shape[1], v_ref.shape[3]
    rows = tall - 2
    inner = pl.ds(1, rows)
    copies = []
    for side in range(2):
        for c in range(3):
            plane = v_ref.at[c, inner, side, :, side * (TILE - 1), :]
            copies.append(pltpu.make_async_copy(plane, z_ref.at[side, c], z_sem.at[side, c]))
            tiles = v_ref.at[c, inner, :, side * (blocks - 1)]
            copies.append(pltpu.make_async_copy(tiles, x_ref.at[side, c], x_sem.at[side, c]))
    for copy in copies:
        copy.start()
    z_even = lax.axis_index("gz") % 2 == 0
    mine, count = lax.axis_index("gx"), lax.axis_size("gx")
    lane = iota((TILE, LANES), 1)
    for copy in copies:
        copy.wait()
    for k in range(3 * rows):
        low, high = z_ref[0, k // rows, k % rows], z_ref[1, k // rows, k % rows]
        z0_ref[k] = jnp.where(z_even, high, low)
        z1_ref[k] = jnp.where(z_even, low, high)
    ends = [jnp.zeros((TILE, LANES), jnp.float32)] * 2
    for k in range(6 * rows):
        for side in range(2):
            tile = pltpu.roll(x_ref[side, k // (2 * rows), k // 2 % rows, k % 2], k + side, 1)
            ends[side] = jnp.where(lane == k, tile, ends[side])
    for g in range(count):
        x_out_ref[g] = jnp.where((mine + 1) % count == g, ends[1], ends[0])


def look_up(total, offset, half):
    position = [half + half * jnp.tanh(a * -0.0625) for a in total]
    knot = [a.astype(jnp.int32) for a in position]
    part = [a - k.astype(jnp.float32) for a, k in zip(position, knot)]
    return [k + offset for k in knot], part


def interpolate(tables, index, part):
    found = [[gather(table, i) for table in tables] for i in index]
    return [[f[k] + p * f[4 + k] for k in range(4)] for f, p in zip(found, part)]


def spread(table_ref):
    return [jnp.broadcast_to(table_ref[k : k + 1, :], (TILE, LANES)) for k in range(8)]


def middle_kernel(rate, v_ref, colormap_hbm, map_hbm, x_in_ref, inner_ref, rest_ref, table_ref, map_ref, pad_ref, index_ref, part_ref, colormap_ref, sem, small):
    tall, blocks = v_ref.shape[1], v_ref.shape[3]
    rows, depth = tall - 2, 2 * TILE
    groups = [range(tall - 2), range(tall - 2, tall)]
    loads = []
    for g, ys in enumerate(groups):
        some = pl.ds(ys[0], len(ys))
        loads.append(
            [
                pltpu.make_async_copy(v_ref.at[:, some, :, b], pad_ref.at[:, some, :, :, LEAD + b, :], sem.at[g, b])
                for b in range(blocks)
            ]
        )
    few = [
        pltpu.make_async_copy(colormap_hbm, colormap_ref, small.at[0]),
        pltpu.make_async_copy(map_hbm, map_ref, small.at[1]),
    ]
    for copy in few:
        copy.start()
    for copies in loads:
        for copy in copies:
            copy.start()
    mine, count = lax.axis_index("gx"), lax.axis_size("gx")
    xl, xh = x_in_ref[(mine + count - 1) % count], x_in_ref[(mine + 1) % count]
    flat = pad_ref.reshape(3 * 2 * tall * TILE * PITCH, LANES)
    for k in range(6 * rows):
        start = ((k // (2 * rows)) * tall + (k // 2) % rows + 1) * depth * PITCH + (k % 2) * TILE * PITCH + LEAD
        flat[pl.ds(start - 1, TILE, stride=PITCH), :] = pltpu.roll(xl, LANES - 1 - k, 1)
        flat[pl.ds(start + blocks, TILE, stride=PITCH), :] = pltpu.roll(xh, (LANES - k) % LANES, 1)
    few[0].wait()
    maps, knots = colormap_ref.shape[0], colormap_ref.shape[2]
    values = jnp.concatenate([colormap_ref[m] for m in range(maps)], axis=1)
    channel, lane = iota(values.shape, 0), iota(values.shape, 1)
    values = jnp.where(channel == 3, values * -rate, values)
    slopes = jnp.where(lane % knots == knots - 1, 0.0, pltpu.roll(values, LANES - 1, 1) - values)
    table_ref[...] = jnp.concatenate([values, slopes], axis=0)
    tables = spread(table_ref)
    few[1].wait()
    lane = iota((TILE, LANES), 1)
    last, first = lane == LANES - 1, lane == 0
    half = 0.5 * (knots - 1)

    def at(c, y, z, move=0):
        return flat[pl.ds(((c * tall + y) * depth + z) * PITCH + LEAD + move, blocks), :]

    def locate(r, zs):
        dx, dy, dz = [], [], []
        for c in range(3):
            own = [at(c, r + 1, z) for z in zs]
            left = [jnp.where(last, at(c, r + 1, z, -1), u) for z, u in zip(zs, own)]
            right = [jnp.where(first, at(c, r + 1, z, 1), u) for z, u in zip(zs, own)]
            left = [pltpu.roll(u, 1, 1) for u in left]
            right = [pltpu.roll(u, LANES - 1, 1) for u in right]
            dx.append([b - a for a, b in zip(left, right)])
            dy.append([at(c, r + 2, z) - at(c, r, z) for z in zs])
            dz.append([None if z in (0, depth - 1) else at(c, r + 1, z + 1) - at(c, r + 1, z - 1) for z in zs])
        n = range(len(zs))
        plane = [dx[0][i] * dx[0][i] + dy[1][i] * dy[1][i] for i in n]
        cross = [dx[1][i] * dy[0][i] for i in n]
        if zs[0] == 0:
            for i, z in enumerate(zs):
                rest_ref[r, i, 0] = plane[i] + (cross[i] + cross[i])
                rest_ref[r, i, 1] = dx[2][i]
                rest_ref[r, i, 2] = dy[2][i]
                for c in range(3):
                    rest_ref[r, i, 3 + c] = at(c, r + 1, abs(z - 1))
            return
        plane = [plane[i] + dz[2][i] * dz[2][i] for i in n]
        cross = [cross[i] + dx[2][i] * dz[0][i] + dy[2][i] * dz[1][i] for i in n]
        total = [a + (b + b) for a, b in zip(plane, cross)]
        offset = map_ref[pl.ds(r, blocks, stride=rows), :] * knots
        index, part = look_up(total, offset, half)
        for z, i, p in zip(zs, index, part):
            index_ref[r, z] = i
            part_ref[r, z] = p

    def paint(r, zs, state):
        sums, log_light, light = state
        shades = interpolate(tables, [index_ref[r, z] for z in zs], [part_ref[r, z] for z in zs])
        for here in shades:
            log_light = log_light + here[3]
            behind = jnp.exp(log_light)
            weight = light - behind
            light = behind
            sums = [a + weight * s for a, s in zip(sums, here)]
        return sums, log_light, light

    zero = jnp.zeros((TILE, LANES), jnp.float32)
    chunks = [range(start, min(start + CHUNK, depth - 1)) for start in range(1, depth - 1, CHUNK)]
    for r in range(rows + 1):
        state = [zero, zero, zero], zero, jnp.ones((TILE, LANES), jnp.float32)
        if r < rows:
            if r % 2 == 0:
                for copy in loads[r // 2]:
                    copy.wait()
            locate(r, (0, depth - 1))
        for zs in chunks:
            if r < rows:
                locate(r, zs)
            if r:
                state = paint(r - 1, zs, state)
        if r:
            for k, value in enumerate(state[0] + [state[1]]):
                inner_ref[r - 1, k] = value


def ends_kernel(knots, z0_ref, z1_ref, inner_ref, rest_ref, table_ref, map_ref, out_ref, y_ref, t_ref):
    rows, blocks = inner_ref.shape[0], inner_ref.shape[2]
    terms = 4 * rows
    tables = spread(table_ref)
    half = 0.5 * (knots - 1)
    z_even = lax.axis_index("gz") % 2 == 0
    every = range(rows)
    total, offset = [], []
    for r in every:
        for side in range(2):
            deep = []
            for c in range(3):
                k = c * rows + r
                halo = jnp.where(z_even, z0_ref[k], z1_ref[k]) if side else jnp.where(z_even, z1_ref[k], z0_ref[k])
                near = rest_ref[r, side, 3 + c]
                deep.append(halo - near if side else near - halo)
            cross = rest_ref[r, side, 1] * deep[0] + rest_ref[r, side, 2] * deep[1]
            total.append(rest_ref[r, side, 0] + deep[2] * deep[2] + (cross + cross))
            offset.append(map_ref[pl.ds(r, blocks, stride=rows), :] * knots)
    index, part = look_up(total, 0, half)
    shades = interpolate(tables, [i + o for i, o in zip(index, offset)], part)
    for r in every:
        front, back = shades[2 * r], shades[2 * r + 1]
        log_front = front[3]
        log_inner = log_front + inner_ref[r, 3]
        log_back = log_inner + back[3]
        past_front, past_inner, past_back = jnp.exp(log_front), jnp.exp(log_inner), jnp.exp(log_back)
        for k in range(3):
            value = (1.0 - past_front) * front[k] + past_front * inner_ref[r, k] + (past_inner - past_back) * back[k]
            y_ref[pl.ds(k * rows + r, blocks, stride=terms), :] = value
        y_ref[pl.ds(3 * rows + r, blocks, stride=terms), :] = log_back
    t_ref[...] = y_ref[...].T
    share = LANES // terms
    parts = [t_ref[pl.ds(j, terms, stride=share), :] for j in range(share)]
    group = iota((terms, LANES), 1) // terms
    bit = share // 2
    while bit:
        for j in range(share):
            if j & bit:
                continue
            one, two = parts[j], parts[j + bit]
            clear = (group & bit) == 0
            parts[j] = jnp.where(clear, one, pltpu.roll(two, bit * terms, 1))
            parts[j + bit] = jnp.where(clear, pltpu.roll(one, LANES - bit * terms, 1), two)
        bit //= 2
    for b in range(blocks):
        out_ref[b * terms : (b + 1) * terms, :] = parts[b]


def compose_kernel(seen_ref, out_ref):
    slabs = seen_ref.shape[0]
    rows = out_ref.shape[1]
    terms = 4 * rows
    share = out_ref.shape[2]
    lane, sub = iota((TILE, LANES), 1), iota((TILE, LANES), 0)
    term = lane % terms
    is_light = term >= 3 * rows
    ahead = jnp.zeros((TILE, LANES), jnp.float32)
    image = jnp.zeros((TILE, LANES), jnp.float32)
    for t in range(slabs // TILE):
        seen = seen_ref[t * TILE : (t + 1) * TILE, :]
        own = jnp.where(is_light, seen, 0.0)
        own = own + pltpu.roll(own, LANES - 2 * rows, 1)
        own = own + pltpu.roll(own, LANES - rows, 1)
        reached = own
        for step in (1, 2, 4):
            reached = reached + jnp.where(sub >= step, pltpu.roll(reached, step, 0), 0.0)
        image = image + jnp.exp(ahead + (reached - own)) * seen
        ahead = ahead + jnp.broadcast_to(reached[TILE - 1 :, :], (TILE, LANES))
    image = jnp.sum(image, axis=0, keepdims=True)
    image = jnp.where(is_light[:1], 1.0 - jnp.exp(ahead[:1]), image)
    image = jnp.broadcast_to(image, (terms, LANES))
    index = (iota((terms, LANES), 1) % share) * terms + iota((terms, LANES), 0)
    image = gather(image, index)
    for k in range(4):
        out_ref[k] = image[k * rows : (k + 1) * rows, :share]


def on_device(velocity, colormap, map_choice):
    slabs = lax.axis_size("gz")
    tall, depth, width = velocity.shape[1:]
    rows = tall - 2
    knots = colormap.shape[1]
    blocks = width // LANES
    rate = 4.0 / (depth * slabs)
    tiles = velocity.reshape(3, tall, 2, TILE, blocks, LANES).transpose(0, 1, 2, 4, 3, 5)
    count = lax.axis_size("gx")
    choice = map_choice.reshape(rows, blocks, LANES).transpose(1, 0, 2).reshape(blocks * rows, LANES)
    hbm = lambda x: pltpu.with_memory_space_constraint(x, pltpu.HBM)
    whole, outside = pl.BlockSpec(memory_space=pltpu.VMEM), pl.BlockSpec(memory_space=pltpu.HBM)
    params = pltpu.CompilerParams(vmem_limit_bytes=16 * 2**20)
    f32 = lambda *shape: jax.ShapeDtypeStruct(shape, jnp.float32)
    z0, z1, x = pl.pallas_call(
        edges_kernel,
        out_shape=(f32(3 * rows, blocks, LANES), f32(3 * rows, blocks, LANES), f32(count, TILE, LANES)),
        in_specs=[outside],
        out_specs=(whole,) * 3,
        scratch_shapes=[
            pltpu.VMEM((2, 3, rows, blocks, LANES), jnp.float32),
            pltpu.VMEM((2, 3, rows, 2, TILE, LANES), jnp.float32),
            pltpu.SemaphoreType.DMA((2, 3)),
            pltpu.SemaphoreType.DMA((2, 3)),
        ],
        compiler_params=params,
        name="edges",
    )(hbm(tiles))
    x = lax.all_to_all(x, "gx", 0, 0, tiled=True)
    z1 = swap(z1, "gz", 1)
    z0 = swap(z0, "gz", 0)
    inner, rest, table, choice = pl.pallas_call(
        functools.partial(middle_kernel, rate),
        out_shape=(
            f32(rows, 4, blocks, LANES),
            f32(rows, 2, 6, blocks, LANES),
            f32(TILE, LANES),
            jax.ShapeDtypeStruct(choice.shape, jnp.int32),
        ),
        in_specs=[outside] * 3 + [whole],
        out_specs=(whole,) * 4,
        scratch_shapes=[
            pltpu.VMEM((3, tall, 2, TILE, PITCH, LANES), jnp.float32),
            pltpu.VMEM((rows, depth, TILE, LANES), jnp.int32),
            pltpu.VMEM((rows, depth, TILE, LANES), jnp.float32),
            pltpu.VMEM((colormap.shape[0], 4, knots), jnp.float32),
            pltpu.SemaphoreType.DMA((2, blocks)),
            pltpu.SemaphoreType.DMA((2,)),
        ],
        compiler_params=params,
        name="middle",
    )(hbm(tiles), hbm(colormap.transpose(0, 2, 1)), hbm(choice), x)
    parts = pl.pallas_call(
        functools.partial(ends_kernel, knots),
        out_shape=f32(slabs, LANES),
        in_specs=[whole] * 6,
        out_specs=whole,
        scratch_shapes=[pltpu.VMEM((LANES, LANES), jnp.float32), pltpu.VMEM((LANES, LANES), jnp.float32)],
        compiler_params=params,
        name="ends",
    )(z0, z1, inner, rest, table, choice)
    seen = lax.all_to_all(parts, "gz", 0, 0, tiled=True)
    return pl.pallas_call(
        compose_kernel,
        out_shape=f32(4, rows, width // slabs),
        in_specs=[whole],
        out_specs=whole,
        compiler_params=params,
        name="compose",
    )(seen)


def solution(mesh):
    placed = (P(None, None, "gz", "gx"), P(), P(None, "gx"))
    return jax.shard_map(
        on_device,
        mesh=mesh,
        in_specs=placed,
        out_specs=P(None, None, ("gx", "gz")),
        check_vma=False,
    )
```

time: 49.1 us -> 49.4 us (level)
  blocking collectives: 26 us -> 33.1 us
  waiting for transfers between devices: 3.93 us -> 0.01 us
  starting transfers between devices: 14.5 us -> 10.7 us
  Pallas kernels: 4.37 us -> 5.25 us
    all_to_all x0 -> x1, blocking collectives: none -> 6.56 us  [on_device(): x = lax.all_to_all(x, 'gx', 0, 0, tiled=True)]
    ppermute x4 -> x2, waiting for transfers between devices: 3.93 us -> 0.01 us  [swap(): return lax.ppermute(x, axis, pairs + [(b, a) for a, b in pairs])]
    ppermute x4 -> x2, starting transfers between devices: 14.5 us -> 10.7 us  [swap(): return lax.ppermute(x, axis, pairs + [(b, a) for a, b in pairs])]
    pallas_call x2 -> x3, Pallas kernels: 3.5 us -> 4.38 us  [the longest x1 2.64 us: on_device(): pl.pallas_call(functools.partial(middle_kernel, rate), out_shape=(f32(row...]
    all_to_all x1, blocking collectives: 26 us -> 26.5 us  [on_device(): seen = lax.all_to_all(parts, 'gz', 0, 0, tiled=True)]
  transfers between devices with their start and end apart: 4 -> 2, of which waited for: 2 -> 0; matrix products, arithmetic and copies ran while one was open for 0% -> 0% of each run, Pallas kernels for 0% -> 5%
where the time goes in v3:
time: 49.4 us; the launch traced here: 49.1 us
  blocking collectives  33.1 us (67%)
  starting transfers between devices  10.7 us (22%)
  Pallas kernels  5.25 us (11%)
    all_to_all x1, blocking collectives, on_device(): seen = lax.all_to_all(parts, 'gz', 0, 0, tiled=True)  26.5 us
    ppermute x2, starting transfers between devices, swap(): return lax.ppermute(x, axis, pairs + [(b, a) for a, b in pairs])  10.7 us
    all_to_all x1, blocking collectives, on_device(): x = lax.all_to_all(x, 'gx', 0, 0, tiled=True)  6.56 us
    pallas_call x1, Pallas kernels, on_device(): pl.pallas_call(functools.partial(middle_kernel, rate), out_shape=(f32(row...  2.64 us
    pallas_call x1, Pallas kernels, on_device(): pl.pallas_call(edges_kernel, out_shape=(f32(3 * rows, blocks, LANES), f32...  1.14 us
  transfers between devices with their start and end apart: 2, of which 0 were waited for; matrix products, arithmetic and copies ran while one was open for 0% of the time, Pallas kernels for 5%

profile of v3, /device:TPU:1, one launch (start us, length us, event | category | flops | bytes accessed | tf_op | source)
XLA Modules:
  0.0 49.1 jit_solution(6261438240896986575)
XLA Ops:
  0.0 1.1 %edges.1 = (f32[12,8,128]{2,1,0:T(8,128)S(1)}, f32[12,8,128]{2,1,0:T(8,128)S(1)}, f32[4,8,128]{2,1,0:T(8,128)S(1)}) custom-call(f32[3,6,2,8,8,128]{5,4,3,2,1,0:T(8,128)} %bitcast.15), custom_call_target="tpu_custom_call" | custom-call | tf_op jit(solution)/shard_map/edges/pallas_call | solution.py:278
  1.2 8.7 %collective-permute-start = (f32[12,8,128]{2,1,0:T(8,128)S(1)}, f32[12,8,128]{2,1,0:T(8,128)S(1)}, u32[]{:S(2)}, u32[]{:S(2)}) collective-permute-start(f32[12,8,128]{2,1,0:T(8,128)S(1)} %get-tuple-element.12), channel_id=1, source_target_pairs={{0,4},{8,12},{16,20},{24,28},{32,36},{40,44},{48,52},{56,60},{64,6... | collective-permute-start | bytes 147464 | tf_op jit(solution)/shard_map/ppermute | solution.py:19
  9.9 1.9 %collective-permute-start.1 = (f32[12,8,128]{2,1,0:T(8,128)S(1)}, f32[12,8,128]{2,1,0:T(8,128)S(1)}, u32[]{:S(2)}, u32[]{:S(2)}) collective-permute-start(f32[12,8,128]{2,1,0:T(8,128)S(1)} %get-tuple-element.13), channel_id=1, source_target_pairs={{4,8},{12,16},{20,24},{28,32},{36,40},{44,48},{52,56},{60,64},{68,... | collective-permute-start | bytes 147464 | tf_op jit(solution)/shard_map/ppermute | solution.py:19
  11.8 6.6 %all_to_all.16.x_in_ref = f32[4,8,128]{2,1,0:T(8,128)S(1)} all-to-all(f32[4,8,128]{2,1,0:T(8,128)S(1)} %get-tuple-element.14), channel_id=1, replica_groups=mesh['gz'=128,'gx'=4] {'gx'}, dimensions={0} | all-to-all | bytes 32768 | tf_op jit(solution)/shard_map/all_to_all | solution.py:292
  18.4 2.6 %middle.1 = (f32[4,4,8,128]{3,2,1,0:T(8,128)S(1)}, f32[4,2,6,8,128]{4,3,2,1,0:T(8,128)S(1)}, f32[8,128]{1,0:T(8,128)S(1)}, s32[32,128]{1,0:T(8,128)S(1)}) custom-call(f32[3,6,2,8,8,128]{5,4,3,2,1,0:T(8,128)} %bitcast.16, f32[8,4,16]{2,1,0:T(4,128)} %bitcast.17, s32[32,128]{1,0:T(8,128)} %bitcast.18, f32[4,8,128]{2,1,0:T(8,128)S(1)} %all_to_all.16.x_in_ref), custom_call_target="tpu_custom_call" | custom-call | tf_op jit(solution)/shard_map/middle/pallas_call | solution.py:295
  21.0 0.0 collective-permute-done.z0_ref
  21.1 0.0 collective-permute-done.1.z1_ref
  21.1 0.6 %ends.1 = f32[128,128]{1,0:T(8,128)S(1)} custom-call(f32[12,8,128]{2,1,0:T(8,128)S(1)} %collective-permute-done.z0_ref, f32[12,8,128]{2,1,0:T(8,128)S(1)} %collective-permute-done.1.z1_ref, f32[4,4,8,128]{3,2,1,0:T(8,128)S(1)} %get-tuple-element.15.inner_ref, f32[4,2,6,8,128]{4,3,2,1,0:T(8,128)S(1)} %get-tuple-element.16.rest_ref, ...), custom_call_target="tpu_custom_call" | custom-call | tf_op jit(solution)/shard_map/ends/pallas_call | solution.py:316
  21.7 26.5 %all_to_all.17 = f32[128,1,128]{2,1,0:T(1,128)S(1)} all-to-all(f32[128,1,128]{2,1,0:T(1,128)S(1)} %bitcast.13), channel_id=1, replica_groups=mesh['gz'=128,'gx'=4] {'gz'}, dimensions={0} | all-to-all | bytes 131072 | tf_op jit(solution)/shard_map/all_to_all | solution.py:325
  48.2 0.9 %compose.1 = f32[4,4,8]{2,1,0:T(4,128)} custom-call(f32[128,128]{1,0:T(8,128)S(1)} %bitcast.14), custom_call_target="tpu_custom_call" | custom-call | tf_op jit(solution)/shard_map/compose/pallas_call | solution.py:326
Async XLA Ops:
  1.2 19.9 %collective-permute-start = (f32[12,8,128]{2,1,0:T(8,128)S(1)}, f32[12,8,128]{2,1,0:T(8,128)S(1)}, u32[]{:S(2)}, u32[]{:S(2)}) collective-permute-start(f32[12,8,128]{2,1,0:T(8,128)S(1)} %get-tuple-element.12), channel_id=1, source_target_pairs={{0,4},{8,12},{16,20},{24,28},{32,36},{40,44},{48,52},{56,60},{64,6... | collective-permute-start | bytes 147464 | tf_op jit(solution)/shard_map/ppermute | solution.py:19
  9.9 11.2 %collective-permute-start.1 = (f32[12,8,128]{2,1,0:T(8,128)S(1)}, f32[12,8,128]{2,1,0:T(8,128)S(1)}, u32[]{:S(2)}, u32[]{:S(2)}) collective-permute-start(f32[12,8,128]{2,1,0:T(8,128)S(1)} %get-tuple-element.13), channel_id=1, source_target_pairs={{4,8},{12,16},{20,24},{28,32},{36,40},{44,48},{52,56},{60,64},{68,... | collective-permute-start | bytes 147464 | tf_op jit(solution)/shard_map/ppermute | solution.py:19
